TPU v7x, 32 devices: a whole 2x2x4 slice. The times are simulated.
32 devices in a mesh: win: 2 (over x), wide: 8 (over z, y), narrow: 2 (over core).
Axes of the slice: x: 2, y: 2, z: 4, core: 2. Of those that a mesh axis runs over, the one named last changes fastest.
Arguments:
- window_data: float32 [384, 128, 256], P(('win', 'wide'), 'narrow'), parts along dimension 0, may hold values from -6 to 6
- factor_one: float32 [256, 48], P(('win', 'narrow')), parts along dimension 0, may hold values from -0.5 to 0.5
- factor_two: float32 [512, 48], P('win'), parts along dimension 0, may hold values from -0.375 to 0.375
- factor_three: float32 [384, 48], P(('win', 'wide')), parts along dimension 0, may hold values from -0.4375 to 0.4375
Outputs:
- basis_one: float32 [256, 48], P(('win', 'narrow')), parts along dimension 0
- basis_two: float32 [512, 48], P('win'), parts along dimension 0
- basis_three: float32 [384, 48], P(('win', 'wide')), parts along dimension 0
- core_unfolded: float32 [48, 4608], P(None, ('win', 'wide', 'narrow')), parts along dimension 1
There are 2 independent parts, one for each index of `win`. A program takes and returns all parts, laid end to end along the dimension named above; each array names one. Nothing has to cross between parts.
All inputs are finite; a program needn't handle non-finite values.
Results may differ from a plain program's by a relative error of at most 0.0003.
Values sent between devices are 32-bit elements; how exact they have to be, the bound alone decides.
No kernel may reach another device: no remote copies, remote signals or barrier semaphores. Data moves between devices by JAX's collectives and lax.ppermute only.
A program may use at most 64 MiB of HBM per device.

v0:
```python
import jax
import jax.numpy as jnp
from jax import lax
from jax.sharding import PartitionSpec as P

highest = lax.Precision.HIGHEST


def contract(form, left, right):
    return jnp.einsum(form, left, right, precision=highest)


def orthonormal(basis, gram):
    lower = jnp.linalg.cholesky(gram)
    return lax.linalg.triangular_solve(lower, basis, left_side=False, lower=True, transpose_a=True)


def full_core(partial_value):
    flat = partial_value.reshape(
        partial_value.shape[0], partial_value.shape[1] * partial_value.shape[2]
    )
    shares = lax.psum_scatter(flat, ("wide", "narrow"), scatter_dimension=1, tiled=True)
    whole = lax.all_gather(shares, ("wide", "narrow"), axis=1, tiled=True)
    return whole.reshape(partial_value.shape)


def on_device(window_data, factor_one, factor_two, factor_three):
    rank = factor_one.shape[1]
    along_two = contract("kij,jb->kib", window_data, factor_two)
    unfold_part = contract("kib,kc->ibc", along_two, factor_three).reshape(
        along_two.shape[1], rank * rank
    )
    unfold_rows = lax.psum_scatter(unfold_part, "wide", scatter_dimension=1, tiled=True)
    weights_one = lax.psum(jnp.dot(unfold_rows.T, factor_one, precision=highest), "narrow")
    product_one = lax.psum(jnp.dot(unfold_rows, weights_one, precision=highest), "wide")
    gram_one = lax.psum(jnp.dot(product_one.T, product_one, precision=highest), "narrow")
    basis_one = orthonormal(product_one, gram_one)
    along_one = contract("kij,ia->kaj", window_data, basis_one)
    core_two = full_core(
        contract("kab,kc->abc", contract("kaj,jb->kab", along_one, factor_two), factor_three)
    )
    spread_two = contract("abc,kc->kab", core_two, factor_three)
    product_two = lax.psum(contract("kaj,kab->jb", along_one, spread_two), ("wide", "narrow"))
    basis_two = orthonormal(product_two, jnp.dot(product_two.T, product_two, precision=highest))
    along_new = contract("kij,jb->kib", window_data, basis_two)
    unfold_three = contract("kib,ia->kab", along_new, basis_one)
    core_three = full_core(contract("kab,kc->abc", unfold_three, factor_three))
    product_three = lax.psum(contract("kab,abc->kc", unfold_three, core_three), "narrow")
    gram_three = lax.psum(jnp.dot(product_three.T, product_three, precision=highest), "wide")
    basis_three = orthonormal(product_three, gram_three)
    core_part = contract("kab,kc->abc", unfold_three, basis_three).reshape(rank, rank * rank)
    core_shares = lax.psum_scatter(core_part, ("wide", "narrow"), scatter_dimension=1, tiled=True)
    return (basis_one, basis_two, basis_three, core_shares)


def solution(mesh):
    return jax.shard_map(
        on_device,
        mesh=mesh,
        in_specs=(
            P(("win", "wide"), "narrow", None),
            P(("win", "narrow"), None),
            P("win", None),
            P(("win", "wide"), None),
        ),
        out_specs=(
            P(("win", "narrow"), None),
            P("win", None),
            P(("win", "wide"), None),
            P(None, ("win", "wide", "narrow")),
        ),
        check_vma=False,
    )
```

profile of v0, /device:TPU:0, one launch (start us, length us, event | category | flops | bytes accessed | tf_op | source)
XLA Modules:
  0.0 505.6 jit_solution(5925950153966513324)
XLA Ops:
  7.2 0.0 reduce-scatter.11.cloned.1.call-start
  7.2 1.3 copy-done
  8.6 3.1 fusion.12
  11.7 2.2 fusion.3
  13.9 0.0 reduce-scatter.13.cloned.1.call-start
  13.9 67.9 %reduce-scatter.11.cloned.1.call-done = f32[64,288]{0,1:T(8,128)} async-done(((f32[64,2304]{0,1:T(8,128)}), f32[64,288]{0,1:T(8,128)}) %reduce-scatter.11.cloned.1.call-update) | async-done | bytes 73744 | tf_op jit(solution)/shard_map/reduce_scatter | solution.py:33
  81.9 1.2 fusion.34
  83.1 3.5 psum.42
  86.6 1.1 fusion.35
  87.7 34.9 %psum.43 = f32[64,48]{0,1:T(8,128)S(1)} all-reduce(f32[64,48]{0,1:T(8,128)S(1)} %fusion.35), channel_id=1, replica_groups=mesh['win'=2,'wide'=8,'narrow'=2] {'wide'}, use_global_device_ids=true, to_apply=%region_2.0 | all-reduce | flops 3072 | bytes 24576 | tf_op jit(solution)/shard_map/psum | solution.py:35
  122.6 0.2 fusion.36
  122.8 3.4 psum.44
  126.2 0.1 copy.26
  126.3 4.4 cholesky.59
  130.7 0.6 compare_reduce_fusion.2
  131.4 0.7 fusion.14
  132.0 3.7 custom-call.11
  135.7 0.2 fusion.25
  136.0 1.1 convolution_bitcast_fusion
  137.1 1.6 fusion
  138.7 3.1 fusion.31
  141.8 2.7 copy.45
  144.5 0.0 reduce-scatter.15.cloned.1.call-start
  144.6 55.5 %reduce-scatter.13.cloned.1.call-done = f32[144,48]{1,0:T(8,128)} async-done(((f32[2304,48]{1,0:T(8,128)}), f32[144,48]{1,0:T(8,128)}) %reduce-scatter.13.cloned.1.call-update) | async-done | bytes 27664
  200.1 1.0 copy.40
  201.0 21.8 %all-gather = f32[16,144,48]{1,2,0:T(8,128)S(1)} all-gather(f32[1,144,48]{1,2,0:T(8,128)S(1)} %bitcast.116), channel_id=1, replica_groups=mesh['win'=2,'wide'=8,'narrow'=2] {'wide','narrow'}, dimensions={0}, use_global_device_ids=true | all-gather | bytes 470016 | tf_op jit(solution)/shard_map/all_gather | solution.py:23
  222.8 0.5 copy.28
  223.3 1.2 reshape.47
  224.4 2.7 reshape.42
  227.2 4.7 convolution_bitcast_fusion.3
  231.9 1.2 convolution_bitcast_fusion.4
  233.1 57.9 %psum.45 = f32[256,48]{0,1:T(8,128)S(1)} all-reduce(f32[256,48]{0,1:T(8,128)S(1)} %convolution_bitcast_fusion.4), channel_id=1, replica_groups=mesh['win'=2,'wide'=8,'narrow'=2] {'wide','narrow'}, use_global_device_ids=true, to_apply=%region_7.0 | all-reduce | flops 12288 | bytes 98304 | tf_op jit(solution)/shard_map/psum | solution.py:43
  291.0 0.2 fusion.37
  291.2 0.1 copy.30
  291.3 4.4 cholesky.70
  295.7 0.6 compare_reduce_fusion.1
  296.4 0.7 fusion.15
  297.0 3.7 custom-call.12
  300.7 0.2 fusion.20
  301.0 2.3 convolution_bitcast_fusion.2
  303.3 2.1 convolution_bitcast_fusion.1
  305.5 2.0 fusion.7
  307.5 1.5 copy.46
  309.0 0.0 reduce-scatter.17.cloned.1.call-start
  309.1 55.5 %reduce-scatter.15.cloned.1.call-done = f32[144,48]{1,0:T(8,128)} async-done(((f32[2304,48]{1,0:T(8,128)}), f32[144,48]{1,0:T(8,128)}) %reduce-scatter.15.cloned.1.call-update) | async-done | bytes 27664
  364.6 1.0 copy.42
  365.5 21.8 %all-gather.1 = f32[16,144,48]{1,2,0:T(8,128)S(1)} all-gather(f32[1,144,48]{1,2,0:T(8,128)S(1)} %bitcast.117), channel_id=1, replica_groups=mesh['win'=2,'wide'=8,'narrow'=2] {'wide','narrow'}, dimensions={0}, use_global_device_ids=true | all-gather | bytes 470016 | tf_op jit(solution)/shard_map/all_gather | solution.py:23
  387.3 0.5 copy.32
  387.8 1.1 reshape.49
  388.9 1.7 reshape.44
  390.7 1.2 convolution_bitcast_fusion.5
  391.9 3.5 psum.46
  395.4 0.2 fusion.38
  395.6 33.0 %psum.47 = f32[48,48]{0,1:T(8,128)S(1)} all-reduce(f32[48,48]{0,1:T(8,128)S(1)} %fusion.38), channel_id=1, replica_groups=mesh['win'=2,'wide'=8,'narrow'=2] {'wide'}, use_global_device_ids=true, to_apply=%region_10.12 | all-reduce | flops 2304 | bytes 18432 | tf_op jit(solution)/shard_map/psum | solution.py:49
  428.6 0.1 copy.35
  428.7 4.4 cholesky.81
  433.1 0.6 compare_reduce_fusion
  433.8 0.7 fusion.16
  434.4 3.7 custom-call.13
  438.1 0.2 fusion.17
  438.3 2.0 fusion.5
  440.3 1.5 copy.47
  441.9 55.6 %reduce-scatter.17.cloned.1.call-done = f32[144,48]{1,0:T(8,128)} async-done(((f32[2304,48]{1,0:T(8,128)}), f32[144,48]{1,0:T(8,128)}) %reduce-scatter.17.cloned.1.call-update) | async-done | bytes 27664
  497.5 1.6 copy.44
  (25 shorter events, 0.2 us)
Async XLA Ops:
  7.2 1.4 copy-start
  7.2 4.5 copy-start.3
  7.2 74.7 %reduce-scatter.11.cloned.1.call-start = ((), (), s32[]{:S(2)}) async-start(), calls=%async_computation.4 | async-start | bytes 1327104 | tf_op jit(solution)/shard_map/reduce_scatter | solution.py:33
  11.7 70.2 %copy-start.7 = (f32[64,48]{0,1:T(8,128)S(1)}, f32[64,48]{0,1:T(8,128)}, u32[]{:S(2)}) copy-start(f32[64,48]{0,1:T(8,128)} %param.6) | copy-start | bytes 36868
  13.9 186.2 %reduce-scatter.13.cloned.1.call-start = ((), (), s32[]{:S(2)}) async-start(), calls=%async_computation.5 | async-start | bytes 1253376
  135.9 1.1 copy-start.1
  136.0 1.1 copy-start.5
  144.5 220.0 %reduce-scatter.15.cloned.1.call-start = ((), (), s32[]{:S(2)}) async-start(), calls=%async_computation.6 | async-start | bytes 1253376
  297.0 6.3 %copy-start.2 = (f32[64,48]{0,1:T(8,128)S(1)}, f32[64,48]{0,1:T(8,128)}, u32[]{:S(2)}) copy-start(f32[64,48]{0,1:T(8,128)} %copy-done.1) | copy-start | bytes 36868
  301.0 4.5 copy-start.4
  309.0 188.4 %reduce-scatter.17.cloned.1.call-start = ((), (), s32[]{:S(2)}) async-start(), calls=%async_computation.7 | async-start | bytes 1253376
  438.3 3.6 copy-start.6
Sparse Core Ops, SparseCore 0:
  14.0 67.8 reduce-scatter.10
  144.7 55.3 reduce-scatter.12
  309.1 55.3 reduce-scatter.14
  442.0 55.4 reduce-scatter.16
where the time goes:
time: 506 us
  waiting for transfers between devices  235 us (46%)
  blocking collectives  180 us (36%)
  matrix products  30.3 us (6%)
  other arithmetic  28.2 us (6%)
  local copies, waits for them, and re-layouts  18.5 us (4%)
  between operations  14.1 us (3%)
    unnamed x7, waiting for transfers between devices  167 us
    reduce_scatter x1, waiting for transfers between devices, on_device(): lax.psum_scatter(unfold_part, 'wide', scatter_dimension=1, tiled=True)  67.9 us
    psum x1, blocking collectives, on_device(): lax.psum(contract('kaj,kab->jb', along_one, spread_two), ('wide', 'narrow'))  57.9 us
    all_gather x2, blocking collectives, full_core(): whole = lax.all_gather(shares, ('wide', 'narrow'), axis=1, tiled=True)  43.6 us
    psum x1, blocking collectives, on_device(): lax.psum(jnp.dot(unfold_rows, weights_one, precision=highest), 'wide')  34.9 us
    psum x1, blocking collectives, on_device(): lax.psum(jnp.dot(product_three.T, product_three, precision=highest), 'wide')  33 us
    dot_general x12, matrix products, contract(): return jnp.einsum(form, left, right, precision=highest)  26.7 us
    another operation x9, other arithmetic, orthonormal(): lower = jnp.linalg.cholesky(gram)  15.2 us
  transfers between devices with their start and end apart: 4, of which 4 were waited for; matrix products, arithmetic and copies ran while one was open for 0% of the time, Pallas kernels for 0%

commit v1 on v0

--- a/solution.py
+++ b/solution.py
@@ -40,7 +40,8 @@
         contract("kab,kc->abc", contract("kaj,jb->kab", along_one, factor_two), factor_three)
     )
     spread_two = contract("abc,kc->kab", core_two, factor_three)
-    product_two = lax.psum(contract("kaj,kab->jb", along_one, spread_two), ("wide", "narrow"))
+    one_axis = lax.psum(contract("kaj,kab->jb", along_one, spread_two), "wide")
+    product_two = lax.psum(one_axis, "narrow")
     basis_two = orthonormal(product_two, jnp.dot(product_two.T, product_two, precision=highest))
     along_new = contract("kij,jb->kib", window_data, basis_two)
     unfold_three = contract("kib,ia->kab", along_new, basis_one)

time: 506 us -> 487 us (0.962)
  blocking collectives: 180 us -> 159 us
    psum x1 -> x2, blocking collectives: 57.9 us -> 36.9 us  [the longest x1 33.4 us: on_device(): one_axis = lax.psum(contract('kaj,kab->jb', along_one, spread_two), 'wide')]
where the time goes in v1:
time: 487 us; the launch traced here: 486 us
  waiting for transfers between devices  236 us (48%)
  blocking collectives  159 us (33%)
  matrix products  30.3 us (6%)
  other arithmetic  28.2 us (6%)
  local copies, waits for them, and re-layouts  18.5 us (4%)
  between operations  14.1 us (3%)
    unnamed x7, waiting for transfers between devices  168 us
    reduce_scatter x1, waiting for transfers between devices, on_device(): lax.psum_scatter(unfold_part, 'wide', scatter_dimension=1, tiled=True)  67.9 us
    all_gather x2, blocking collectives, full_core(): whole = lax.all_gather(shares, ('wide', 'narrow'), axis=1, tiled=True)  43.3 us
    psum x1, blocking collectives, on_device(): lax.psum(jnp.dot(unfold_rows, weights_one, precision=highest), 'wide')  34.9 us
    psum x1, blocking collectives, on_device(): one_axis = lax.psum(contract('kaj,kab->jb', along_one, spread_two), 'wide')  33.4 us
    psum x1, blocking collectives, on_device(): lax.psum(jnp.dot(product_three.T, product_three, precision=highest), 'wide')  33 us
    dot_general x12, matrix products, contract(): return jnp.einsum(form, left, right, precision=highest)  26.7 us
    another operation x9, other arithmetic, orthonormal(): lower = jnp.linalg.cholesky(gram)  15.2 us
  transfers between devices with their start and end apart: 4, of which 4 were waited for; matrix products, arithmetic and copies ran while one was open for 0% of the time, Pallas kernels for 0%

profile of v1, /device:TPU:0, one launch (start us, length us, event | category | flops | bytes accessed | tf_op | source)
XLA Modules:
  0.0 485.8 jit_solution(5804607225270512968)
XLA Ops:
  7.2 1.3 copy-done
  8.6 3.1 fusion.12
  11.7 2.2 fusion.3
  13.9 0.0 reduce-scatter.13.cloned.1.call-start
  13.9 67.9 %reduce-scatter.11.cloned.1.call-done = f32[64,288]{0,1:T(8,128)} async-done(((f32[64,2304]{0,1:T(8,128)}), f32[64,288]{0,1:T(8,128)}) %reduce-scatter.11.cloned.1.call-update) | async-done | bytes 73744 | tf_op jit(solution)/shard_map/reduce_scatter | solution.py:33
  81.9 1.2 fusion.34
  83.1 3.5 psum.49
  86.6 1.1 fusion.35
  87.7 34.9 %psum.50 = f32[64,48]{0,1:T(8,128)S(1)} all-reduce(f32[64,48]{0,1:T(8,128)S(1)} %fusion.35), channel_id=1, replica_groups=mesh['win'=2,'wide'=8,'narrow'=2] {'wide'}, use_global_device_ids=true, to_apply=%region_2.0 | all-reduce | flops 3072 | bytes 24576 | tf_op jit(solution)/shard_map/psum | solution.py:35
  122.6 0.2 fusion.36
  122.8 3.4 psum.51
  126.2 0.1 copy.26
  126.3 4.4 cholesky.59
  130.7 0.6 compare_reduce_fusion.2
  131.4 0.7 fusion.14
  132.0 3.7 custom-call.11
  135.7 0.2 fusion.25
  136.0 1.1 convolution_bitcast_fusion
  137.1 1.6 fusion
  138.7 3.1 fusion.31
  141.8 2.7 copy.45
  144.5 0.0 reduce-scatter.15.cloned.1.call-start
  144.6 55.5 %reduce-scatter.13.cloned.1.call-done = f32[144,48]{1,0:T(8,128)} async-done(((f32[2304,48]{1,0:T(8,128)}), f32[144,48]{1,0:T(8,128)}) %reduce-scatter.13.cloned.1.call-update) | async-done | bytes 27664
  200.1 1.0 copy.40
  201.0 21.8 %all-gather = f32[16,144,48]{1,2,0:T(8,128)S(1)} all-gather(f32[1,144,48]{1,2,0:T(8,128)S(1)} %bitcast.116), channel_id=1, replica_groups=mesh['win'=2,'wide'=8,'narrow'=2] {'wide','narrow'}, dimensions={0}, use_global_device_ids=true | all-gather | bytes 470016 | tf_op jit(solution)/shard_map/all_gather | solution.py:23
  222.8 0.5 copy.28
  223.3 1.2 reshape.47
  224.4 2.7 reshape.42
  227.2 4.7 convolution_bitcast_fusion.3
  231.9 1.2 convolution_bitcast_fusion.4
  233.1 33.4 %psum.52 = f32[256,48]{0,1:T(8,128)S(1)} all-reduce(f32[256,48]{0,1:T(8,128)S(1)} %convolution_bitcast_fusion.4), channel_id=1, replica_groups=mesh['win'=2,'wide'=8,'narrow'=2] {'wide'}, use_global_device_ids=true, to_apply=%region_7.0 | all-reduce | flops 12288 | bytes 98304 | tf_op jit(solution)/shard_map/psum | solution.py:43
  266.5 3.5 psum.53
  270.0 0.2 fusion.37
  270.2 0.1 copy.30
  270.3 4.4 cholesky.70
  274.7 0.6 compare_reduce_fusion.1
  275.4 0.7 fusion.15
  276.1 3.7 custom-call.12
  279.7 0.3 fusion.20
  280.0 2.3 convolution_bitcast_fusion.2
  282.3 2.1 convolution_bitcast_fusion.1
  284.5 2.0 fusion.7
  286.5 1.5 copy.46
  288.0 0.3 reduce-scatter.17.cloned.1.call-start
  288.3 56.7 %reduce-scatter.15.cloned.1.call-done = f32[144,48]{1,0:T(8,128)} async-done(((f32[2304,48]{1,0:T(8,128)}), f32[144,48]{1,0:T(8,128)}) %reduce-scatter.15.cloned.1.call-update) | async-done | bytes 27664
  345.0 1.0 copy.42
  346.0 21.6 %all-gather.1 = f32[16,144,48]{1,2,0:T(8,128)S(1)} all-gather(f32[1,144,48]{1,2,0:T(8,128)S(1)} %bitcast.117), channel_id=1, replica_groups=mesh['win'=2,'wide'=8,'narrow'=2] {'wide','narrow'}, dimensions={0}, use_global_device_ids=true | all-gather | bytes 470016 | tf_op jit(solution)/shard_map/all_gather | solution.py:23
  367.6 0.5 copy.32
  368.0 1.1 reshape.49
  369.2 1.7 reshape.44
  370.9 1.2 convolution_bitcast_fusion.5
  372.2 3.5 psum.54
  375.6 0.2 fusion.38
  375.9 33.0 %psum.55 = f32[48,48]{0,1:T(8,128)S(1)} all-reduce(f32[48,48]{0,1:T(8,128)S(1)} %fusion.38), channel_id=1, replica_groups=mesh['win'=2,'wide'=8,'narrow'=2] {'wide'}, use_global_device_ids=true, to_apply=%region_11.13 | all-reduce | flops 2304 | bytes 18432 | tf_op jit(solution)/shard_map/psum | solution.py:50
  408.9 0.1 copy.35
  409.0 4.4 cholesky.81
  413.4 0.6 compare_reduce_fusion
  414.0 0.7 fusion.16
  414.7 3.7 custom-call.13
  418.4 0.2 fusion.17
  418.6 2.0 fusion.5
  420.6 1.5 copy.47
  422.1 55.6 %reduce-scatter.17.cloned.1.call-done = f32[144,48]{1,0:T(8,128)} async-done(((f32[2304,48]{1,0:T(8,128)}), f32[144,48]{1,0:T(8,128)}) %reduce-scatter.17.cloned.1.call-update) | async-done | bytes 27664
  477.7 1.6 copy.44
  (26 shorter events, 0.3 us)
Async XLA Ops:
  7.2 1.4 copy-start
  7.2 4.5 copy-start.3
  7.2 74.7 %reduce-scatter.11.cloned.1.call-start = ((), (), s32[]{:S(2)}) async-start(), calls=%async_computation.4 | async-start | bytes 1327104 | tf_op jit(solution)/shard_map/reduce_scatter | solution.py:33
  11.7 70.2 %copy-start.7 = (f32[64,48]{0,1:T(8,128)S(1)}, f32[64,48]{0,1:T(8,128)}, u32[]{:S(2)}) copy-start(f32[64,48]{0,1:T(8,128)} %param.6) | copy-start | bytes 36868
  13.9 186.2 %reduce-scatter.13.cloned.1.call-start = ((), (), s32[]{:S(2)}) async-start(), calls=%async_computation.5 | async-start | bytes 1253376
  135.9 1.1 copy-start.1
  136.0 1.1 copy-start.5
  144.5 200.5 %reduce-scatter.15.cloned.1.call-start = ((), (), s32[]{:S(2)}) async-start(), calls=%async_computation.6 | async-start | bytes 1253376
  276.0 6.3 %copy-start.2 = (f32[64,48]{0,1:T(8,128)S(1)}, f32[64,48]{0,1:T(8,128)}, u32[]{:S(2)}) copy-start(f32[64,48]{0,1:T(8,128)} %copy-done.1) | copy-start | bytes 36868
  280.0 4.5 copy-start.4
  288.0 189.7 %reduce-scatter.17.cloned.1.call-start = ((), (), s32[]{:S(2)}) async-start(), calls=%async_computation.7 | async-start | bytes 1253376
  418.5 3.6 copy-start.6
Sparse Core Ops, SparseCore 0:
  14.0 67.8 reduce-scatter.10
  144.7 55.3 reduce-scatter.12
  288.2 56.8 reduce-scatter.14
  422.2 55.4 reduce-scatter.16
